TPU v7x, 256 devices: a whole 4x4x8 slice. The times are simulated.
256 devices in a mesh: row: 64 (over y, z, core), col: 4 (over x).
Axes of the slice: x: 4, y: 4, z: 8, core: 2. Of those that a mesh axis runs over, the one named last changes fastest.
Arguments:
- trailing: float32 [65536, 4096], P('row', 'col'), may hold values from -6 to 6
- panel_y: float32 [65536, 256], P(('row', 'col')), may hold values from -0.1875 to 0.1875
- panel_t: float32 [16384, 256], P('row'), may hold values from 0.5 to 1.5
- tree_v: float32 [3, 16384, 256], P(None, 'row'), may hold values from -0.375 to 0.375, as said below
- tree_t: float32 [3, 16384, 256], P(None, 'row'), may hold values from 0.5 to 1.5, as said below
Outputs:
- updated: float32 [65536, 4096], P('row', 'col')
Inputs may be any that keep to these rules, and one draw needn't show every extreme that they name: For each level l, the blocks of 256 rows that tree_v[l] holds for two tile rows that differ only in bit l are equal. For each level l, the blocks of 256 rows that tree_t[l] holds for two tile rows that differ only in bit l are equal.
All inputs are finite; a program needn't handle non-finite values.
Results may differ from a plain program's by a relative error of at most 0.0001.
Values sent between devices are 32-bit elements; how exact they have to be, the bound alone decides.
No kernel may reach another device: no remote copies, remote signals or barrier semaphores. Data moves between devices by JAX's collectives and lax.ppermute only.
A program may use at most 64 MiB of HBM per device.

v0:
```python
import math
import jax
import jax.numpy as jnp
from jax import lax
from jax.sharding import PartitionSpec as P


def from_partner(block, axis, bit):
    count = lax.axis_size(axis)
    route = []
    for low in range(count):
        high = low | 1 << bit
        if high != low and high < count:
            route += [(low, high), (high, low)]
    return lax.ppermute(block, axis, route)


def unit_lower(values):
    rows = jnp.arange(values.shape[0])[:, None]
    cols = jnp.arange(values.shape[1])[None, :]
    return jnp.where(
        rows > cols, values, jnp.where(rows == cols, jnp.float32(1.0), jnp.float32(0.0))
    )


def triangle_factor(values):
    width = values.shape[-1]
    rows = jnp.arange(width)[:, None]
    cols = jnp.arange(width)[None, :]
    scale = 2.0 / math.sqrt(width)
    return jnp.where(
        rows == cols, values, jnp.where(cols > rows, (values - 1.0) * scale, jnp.float32(0.0))
    )


def upper_part(values):
    width = values.shape[-1]
    rows = jnp.arange(width)[:, None]
    cols = jnp.arange(width)[None, :]
    return jnp.where(cols >= rows, values, jnp.float32(0.0))


def pair_update(first, second, vees, tees):
    highest = lax.Precision.HIGHEST
    summed = first + jnp.einsum("kb,kn->bn", vees, second, precision=highest)
    factor = jnp.einsum("kb,kn->bn", tees, summed, precision=highest)
    return (first - factor, second - jnp.dot(vees, factor, precision=highest))


def per_device(trailing, panel_y, panel_t, tree_v, tree_t):
    highest = lax.Precision.HIGHEST
    width = panel_t.shape[1]
    columns = trailing.shape[1]
    half = columns // 2
    gathered = lax.all_gather(panel_y, "col", axis=0, tiled=True)
    lower = unit_lower(gathered)
    proj = jnp.einsum("mb,mn->bn", lower, trailing, precision=highest)
    weight = jnp.einsum("kb,kn->bn", triangle_factor(panel_t), proj, precision=highest)
    local = trailing - jnp.dot(lower, weight, precision=highest)
    top = local[:width]
    rest = local[width:]
    position = lax.axis_index("row")
    for level in range(tree_v.shape[0]):
        leader = position >> level & 1 == 0
        vees = upper_part(tree_v[level])
        tees = triangle_factor(tree_t[level])
        left = top[:, :half]
        right = top[:, half:]
        outgoing = jnp.where(leader, right, left)
        incoming = from_partner(outgoing, "row", level)
        first = jnp.where(leader, left, incoming)
        second = jnp.where(leader, incoming, right)
        new_first, new_second = pair_update(first, second, vees, tees)
        sendback = jnp.where(leader, new_second, new_first)
        returned = from_partner(sendback, "row", level)
        top = jnp.where(
            leader,
            jnp.concatenate([new_first, returned], axis=1),
            jnp.concatenate([returned, new_second], axis=1),
        )
    return jnp.concatenate([top, rest], axis=0)


def solution(mesh):
    placed = (
        P("row", "col"),
        P(("row", "col"), None),
        P("row", None),
        P(None, "row", None),
        P(None, "row", None),
    )
    return jax.shard_map(
        per_device, mesh=mesh, in_specs=placed, out_specs=P("row", "col"), check_vma=False
    )
```

profile of v0, /device:TPU:8, one launch (start us, length us, event | category | flops | bytes accessed | tf_op | source)
XLA Modules:
  0.0 161.7 jit_solution(15290932979044176380)
XLA Ops:
  6.5 0.7 all-gather.2.cloned.1.call-update
  7.3 5.3 %copy.6 = f32[1024,1024]{0,1:T(8,128)} copy(f32[1024,1024]{1,0:T(8,128)} %param.5) | data formatting | bytes 8388608 | tf_op args[0]
  12.6 26.1 %all-gather.2.cloned.1.call-done = f32[1024,256]{1,0:T(8,128)} async-done(((f32[256,256]{1,0:T(8,128)}), f32[1024,256]{1,0:T(8,128)}) %all-gather.2.cloned.1.call-update) | async-done | bytes 1048592 | tf_op jit(solution)/shard_map/all_gather | solution.py:55
  38.7 6.0 %fusion = f32[256,1024]{1,0:T(8,128)S(1)} fusion(f32[1024,1024]{1,0:T(8,128)} %param.5, f32[1024,256]{1,0:T(8,128)} %all-gather.2.cloned.1.call-done), kind=kOutput, calls=%fused_computation.14 | convolution fusion | flops 3222274048 | bytes 6291456 | tf_op jit(solution)/shard_map/mb,mn->bn/dot_general | solution.py:57
  44.7 1.1 fusion.17
  45.8 3.8 %convolution_subtract_fusion = f32[1024,1024]{0,1:T(8,128)S(1)} fusion(f32[1024,1024]{0,1:T(8,128)S(1)} %copy-done.1, f32[256,1024]{1,0:T(8,128)S(1)} %fusion.17, f32[1024,256]{1,0:T(8,128)S(1)} %copy-done.2), kind=kOutput, calls=%fused_computation.1 | convolution fusion | flops 3223322624 | bytes 10485760 | tf_op jit(solution)/shard_map/dot_general | solution.py:59
  49.6 0.1 slice_select_fusion.7
  49.9 1.9 %collective-permute-done = f32[256,512]{0,1:T(8,128)S(1)} collective-permute-done((f32[256,512]{0,1:T(8,128)S(1)}, f32[256,512]{0,1:T(8,128)S(1)}, u32[]{:S(2)}, u32[]{:S(2)}) %collective-permute-start) | collective-permute-done | bytes 524320 | tf_op jit(solution)/shard_map/ppermute | solution.py:15
  51.8 0.6 convolution_add_fusion.2
  52.4 1.8 %fusion.13 = f32[256,512]{1,0:T(8,128)S(1)} fusion(f32[256,512]{0,1:T(8,128)S(1)} %convolution_add_fusion.2, f32[3,256,256]{2,1,0:T(8,128)} %param.9), kind=kOutput, calls=%fused_computation.45 | convolution fusion | flops 403046400 | bytes 1310720 | tf_op jit(solution)/shard_map/kb,kn->bn/dot_general | solution.py:46
  54.3 0.2 copy.7
  54.5 3.0 %broadcast_select_fusion = (f32[256,512]{0,1:T(8,128)}, f32[256,512]{0,1:T(8,128)S(1)}, f32[256,512]{0,1:T(8,128)S(1)}) fusion(pred[]{:T(512)S(6)} %eq.100, f32[256,512]{0,1:T(8,128)S(1)} %copy.7, f32[256,512]{0,1:T(8,128)S(1)} %collective-permute-done, f32[1024,1024]{0,1:T(8,128)} %copy-done, f32[256,512]{1,0:T(8,128)S(1)} %fusion.13, ...), kind=kOutput, calls=%fused_computation.57 | convolution fusion | flops 403439616 | bytes 4456449 | tf_op jit(solution)/shard_map/dot_general | solution.py:47
  57.5 0.1 collective-permute-start.1
  57.6 2.0 %collective-permute-done.1 = f32[256,512]{0,1:T(8,128)S(1)} collective-permute-done((f32[256,512]{0,1:T(8,128)}, f32[256,512]{0,1:T(8,128)S(1)}, u32[]{:S(2)}, u32[]{:S(2)}) %collective-permute-start.1) | collective-permute-done | bytes 524320 | tf_op jit(solution)/shard_map/ppermute | solution.py:15
  59.8 1.8 %collective-permute-start.2 = (f32[256,512]{0,1:T(8,128)S(1)}, f32[256,512]{0,1:T(8,128)S(1)}, u32[]{:S(2)}, u32[]{:S(2)}) collective-permute-start(f32[256,512]{0,1:T(8,128)S(1)} %slice_select_fusion.4), channel_id=1, source_target_pairs={{0,8},{8,0},{4,12},{12,4},{16,24},{24,16},{20,28},{28,20},{32,40},... | collective-permute-start | bytes 1572872 | tf_op jit(solution)/shard_map/ppermute | solution.py:15
  61.6 12.4 %collective-permute-done.2 = f32[256,512]{0,1:T(8,128)S(1)} collective-permute-done((f32[256,512]{0,1:T(8,128)S(1)}, f32[256,512]{0,1:T(8,128)S(1)}, u32[]{:S(2)}, u32[]{:S(2)}) %collective-permute-start.2) | collective-permute-done | bytes 524320 | tf_op jit(solution)/shard_map/ppermute | solution.py:15
  74.0 0.6 convolution_add_fusion.1
  74.6 1.8 %fusion.10 = f32[256,512]{1,0:T(8,128)S(1)} fusion(f32[256,512]{0,1:T(8,128)S(1)} %convolution_add_fusion.1, f32[3,256,256]{2,1,0:T(8,128)} %param.9), kind=kOutput, calls=%fused_computation.39 | convolution fusion | flops 403046400 | bytes 1310720 | tf_op jit(solution)/shard_map/kb,kn->bn/dot_general | solution.py:46
  76.5 0.2 copy.9
  76.7 2.1 %broadcast_select_fusion.1 = (f32[256,512]{0,1:T(8,128)}, f32[256,512]{0,1:T(8,128)}, f32[256,512]{0,1:T(8,128)}) fusion(pred[]{:T(512)S(6)} %eq.99, f32[256,512]{0,1:T(8,128)S(1)} %copy.9, f32[256,512]{0,1:T(8,128)S(1)} %collective-permute-done.2, f32[256,1024]{0,1:T(8,128)S(1)} %maximum_select_fusion, f32[256,512]{1,0:T(8,128)S(1)} %fusion.10, ...), kind=kOutput, calls=%fused_computation.58 | convolution fusion | flops 403439616 | bytes 4456449 | tf_op jit(solution)/shard_map/dot_general | solution.py:47
  78.8 1.5 collective-permute-start.3
  80.3 11.8 %collective-permute-done.3 = f32[256,512]{0,1:T(8,128)S(1)} collective-permute-done((f32[256,512]{0,1:T(8,128)}, f32[256,512]{0,1:T(8,128)S(1)}, u32[]{:S(2)}, u32[]{:S(2)}) %collective-permute-start.3) | collective-permute-done | bytes 524320 | tf_op jit(solution)/shard_map/ppermute | solution.py:15
  92.1 1.3 maximum_select_fusion.1
  93.5 2.6 %collective-permute-start.4 = (f32[256,512]{0,1:T(8,128)S(1)}, f32[256,512]{0,1:T(8,128)S(1)}, u32[]{:S(2)}, u32[]{:S(2)}) collective-permute-start(f32[256,512]{0,1:T(8,128)S(1)} %slice_select_fusion.1), channel_id=1, source_target_pairs={{0,16},{16,0},{4,20},{20,4},{8,24},{24,8},{12,28},{28,12},{32,48},... | collective-permute-start | bytes 1572872 | tf_op jit(solution)/shard_map/ppermute | solution.py:15
  96.1 21.8 %collective-permute-done.4 = f32[256,512]{0,1:T(8,128)S(1)} collective-permute-done((f32[256,512]{0,1:T(8,128)S(1)}, f32[256,512]{0,1:T(8,128)S(1)}, u32[]{:S(2)}, u32[]{:S(2)}) %collective-permute-start.4) | collective-permute-done | bytes 524320 | tf_op jit(solution)/shard_map/ppermute | solution.py:15
  118.0 0.6 convolution_add_fusion
  118.6 1.8 %fusion.7 = f32[256,512]{1,0:T(8,128)S(1)} fusion(f32[256,512]{0,1:T(8,128)S(1)} %convolution_add_fusion, f32[3,256,256]{2,1,0:T(8,128)} %param.9), kind=kOutput, calls=%fused_computation.33 | convolution fusion | flops 403046400 | bytes 1310720 | tf_op jit(solution)/shard_map/kb,kn->bn/dot_general | solution.py:46
  120.4 0.2 copy.11
  120.6 1.0 broadcast_select_fusion.2
  121.8 25.0 %collective-permute-done.5 = f32[256,512]{0,1:T(8,128)S(1)} collective-permute-done((f32[256,512]{0,1:T(8,128)S(1)}, f32[256,512]{0,1:T(8,128)S(1)}, u32[]{:S(2)}, u32[]{:S(2)}) %collective-permute-start.5) | collective-permute-done | bytes 524320 | tf_op jit(solution)/shard_map/ppermute | solution.py:15
  146.9 2.6 %pad_maximum_fusion = f32[1024,1024]{0,1:T(8,128)} fusion(f32[768,1024]{0,1:T(8,128)S(1)} %slice-done, f32[256,1024]{0,1:T(8,128)S(1)} %maximum_select_fusion.2), kind=kLoop, calls=%fused_computation | loop fusion | flops 1048576 | bytes 8388608 | tf_op jit(solution)/shard_map/concatenate | solution.py:81
  149.5 5.3 %copy.13 = f32[1024,1024]{1,0:T(8,128)} copy(f32[1024,1024]{0,1:T(8,128)} %pad_maximum_fusion) | data formatting | bytes 8388608 | tf_op jit(solution)/shard_map/concatenate | solution.py:81
  (19 shorter events, 0.6 us)
Async XLA Ops:
  6.5 32.1 %all-gather.2.cloned.1.call-start = ((), (), s32[]{:S(2)}) async-start(), calls=%async_computation | async-start | bytes 1310720 | tf_op jit(solution)/shard_map/all_gather | solution.py:55
  12.6 32.1 %copy-start.4 = (f32[256,256]{1,0:T(8,128)S(1)}, f32[256,256]{1,0:T(8,128)}, u32[]{:S(2)}) copy-start(f32[256,256]{1,0:T(8,128)} %param.7) | copy-start | bytes 786436
  38.7 7.1 %copy-start.1 = (f32[1024,1024]{0,1:T(8,128)S(1)}, f32[1024,1024]{0,1:T(8,128)}, u32[]{:S(2)}) copy-start(f32[1024,1024]{0,1:T(8,128)} %copy.6) | copy-start | bytes 12582916
  38.7 7.1 %copy-start.2 = (f32[1024,256]{1,0:T(8,128)S(1)}, f32[1024,256]{1,0:T(8,128)}, u32[]{:S(2)}) copy-start(f32[1024,256]{1,0:T(8,128)} %all-gather.2.cloned.1.call-done) | copy-start | bytes 3145732
  45.8 6.0 %copy-start.3 = (f32[3,256,256]{2,1,0:T(8,128)S(1)}, f32[3,256,256]{2,1,0:T(8,128)}, u32[]{:S(2)}) copy-start(f32[3,256,256]{2,1,0:T(8,128)} %param.8) | copy-start | bytes 2359300
  49.6 2.1 %copy-start = (f32[1024,1024]{0,1:T(8,128)}, f32[1024,1024]{0,1:T(8,128)S(1)}, u32[]{:S(2)}) copy-start(f32[1024,1024]{0,1:T(8,128)S(1)} %convolution_subtract_fusion) | copy-start | bytes 12582916
  49.8 2.0 %collective-permute-start = (f32[256,512]{0,1:T(8,128)S(1)}, f32[256,512]{0,1:T(8,128)S(1)}, u32[]{:S(2)}, u32[]{:S(2)}) collective-permute-start(f32[256,512]{0,1:T(8,128)S(1)} %slice_select_fusion.7), channel_id=1, source_target_pairs={{0,4},{4,0},{8,12},{12,8},{16,20},{20,16},{24,28},{28,24},{32,36},... | collective-permute-start | bytes 1572872 | tf_op jit(solution)/shard_map/ppermute | solution.py:15
  57.5 2.1 %collective-permute-start.1 = (f32[256,512]{0,1:T(8,128)}, f32[256,512]{0,1:T(8,128)S(1)}, u32[]{:S(2)}, u32[]{:S(2)}) collective-permute-start(f32[256,512]{0,1:T(8,128)} %get-tuple-element.9), channel_id=1, source_target_pairs={{0,4},{4,0},{8,12},{12,8},{16,20},{20,16},{24,28},{28,24},{32,36},... | collective-permute-start | bytes 1572872 | tf_op jit(solution)/shard_map/ppermute | solution.py:15
  59.8 14.2 %collective-permute-start.2 = (f32[256,512]{0,1:T(8,128)S(1)}, f32[256,512]{0,1:T(8,128)S(1)}, u32[]{:S(2)}, u32[]{:S(2)}) collective-permute-start(f32[256,512]{0,1:T(8,128)S(1)} %slice_select_fusion.4), channel_id=1, source_target_pairs={{0,8},{8,0},{4,12},{12,4},{16,24},{24,16},{20,28},{28,20},{32,40},... | collective-permute-start | bytes 1572872 | tf_op jit(solution)/shard_map/ppermute | solution.py:15
  78.8 13.3 %collective-permute-start.3 = (f32[256,512]{0,1:T(8,128)}, f32[256,512]{0,1:T(8,128)S(1)}, u32[]{:S(2)}, u32[]{:S(2)}) collective-permute-start(f32[256,512]{0,1:T(8,128)} %get-tuple-element.7), channel_id=1, source_target_pairs={{0,8},{8,0},{4,12},{12,4},{16,24},{24,16},{20,28},{28,20},{32,40},... | collective-permute-start | bytes 1572872 | tf_op jit(solution)/shard_map/ppermute | solution.py:15
  93.5 24.5 %collective-permute-start.4 = (f32[256,512]{0,1:T(8,128)S(1)}, f32[256,512]{0,1:T(8,128)S(1)}, u32[]{:S(2)}, u32[]{:S(2)}) collective-permute-start(f32[256,512]{0,1:T(8,128)S(1)} %slice_select_fusion.1), channel_id=1, source_target_pairs={{0,16},{16,0},{4,20},{20,4},{8,24},{24,8},{12,28},{28,12},{32,48},... | collective-permute-start | bytes 1572872 | tf_op jit(solution)/shard_map/ppermute | solution.py:15
  121.7 25.2 %slice-start = ((f32[1024,1024]{0,1:T(8,128)}), f32[768,1024]{0,1:T(8,128)S(1)}, s32[]{:S(2)}) async-start(f32[1024,1024]{0,1:T(8,128)} %copy-done), calls=%async_computation.1 | async-start | bytes 6291456 | tf_op jit(solution)/shard_map/slice | solution.py:61
  121.7 25.1 %collective-permute-start.5 = (f32[256,512]{0,1:T(8,128)S(1)}, f32[256,512]{0,1:T(8,128)S(1)}, u32[]{:S(2)}, u32[]{:S(2)}) collective-permute-start(f32[256,512]{0,1:T(8,128)S(1)} %get-tuple-element.5), channel_id=1, source_target_pairs={{0,16},{16,0},{4,20},{20,4},{8,24},{24,8},{12,28},{28,12},{32,48},... | collective-permute-start | bytes 1572872 | tf_op jit(solution)/shard_map/ppermute | solution.py:15
Sparse Core Ops, SparseCore 0:
  9.1 29.4 all-gather.1
where the time goes:
time: 162 us
  waiting for transfers between devices  102 us (63%)
  matrix products  24.4 us (15%)
  between operations  13.6 us (8%)
  local copies, waits for them, and re-layouts  11.3 us (7%)
  starting transfers between devices  6.33 us (4%)
  other arithmetic  4.38 us (3%)
    ppermute x6, waiting for transfers between devices, from_partner(): return lax.ppermute(block, axis, route)  74.9 us
    all_gather x1, waiting for transfers between devices, per_device(): gathered = lax.all_gather(panel_y, 'col', axis=0, tiled=True)  26.1 us
    ppermute x6, starting transfers between devices, from_partner(): return lax.ppermute(block, axis, route)  6.32 us
    dot_general x3, matrix products, pair_update(): return (first - factor, second - jnp.dot(vees, factor, precision=highest))  6.15 us
    dot_general x1, matrix products, per_device(): proj = jnp.einsum('mb,mn->bn', lower, trailing, precision=highest)  6.04 us
    dot_general x3, matrix products, pair_update(): factor = jnp.einsum('kb,kn->bn', tees, summed, precision=highest)  5.51 us
    unnamed x11, local copies, waits for them, and re-layouts  5.37 us
    concatenate x1, local copies, waits for them, and re-layouts, per_device(): return jnp.concatenate([top, rest], axis=0)  5.34 us
  transfers between devices with their start and end apart: 7, of which 7 were waited for; matrix products, arithmetic and copies ran while one was open for 3% of the time, Pallas kernels for 0%

commit v1 on v0

--- a/solution.py
+++ b/solution.py
@@ -52,7 +52,9 @@
     width = panel_t.shape[1]
     columns = trailing.shape[1]
     half = columns // 2
-    gathered = lax.all_gather(panel_y, "col", axis=0, tiled=True)
+    gathered = jnp.concatenate(
+        lax.all_to_all(jnp.stack([panel_y] * lax.axis_size("col")), "col", 0, 0), axis=0
+    )
     lower = unit_lower(gathered)
     proj = jnp.einsum("mb,mn->bn", lower, trailing, precision=highest)
     weight = jnp.einsum("kb,kn->bn", triangle_factor(panel_t), proj, precision=highest)

time: 162 us -> 139 us (0.86)
  waiting for transfers between devices: 102 us -> 84.6 us
  between operations: 13.6 us -> 0.22 us
  starting transfers between devices: 6.33 us -> 11.9 us
  local copies, waits for them, and re-layouts: 11.3 us -> 13.3 us
    all_gather x1 -> x0, waiting for transfers between devices: 26.1 us -> none  [per_device(): gathered = lax.all_gather(panel_y, 'col', axis=0, tiled=True)]
    all_to_all x0 -> x1, waiting for transfers between devices: none -> 9.75 us  [per_device(): lax.all_to_all(jnp.stack([panel_y] * lax.axis_size('col')), 'col', 0, 0)]
    all_to_all x0 -> x1, starting transfers between devices: none -> 4.29 us  [per_device(): lax.all_to_all(jnp.stack([panel_y] * lax.axis_size('col')), 'col', 0, 0)]
    another operation x0 -> x1, local copies, waits for them, and re-layouts: none -> 2.01 us  [per_device(): jnp.stack([panel_y] * lax.axis_size('col'))]
    unnamed x11 -> x9, local copies, waits for them, and re-layouts: 5.37 us -> 5.36 us
  transfers between devices with their start and end apart: 7 -> 7, of which waited for: 7 -> 7; matrix products, arithmetic and copies ran while one was open for 3% -> 4% of each run, Pallas kernels for 0% -> 0%
where the time goes in v1:
time: 139 us
  waiting for transfers between devices  84.6 us (61%)
  matrix products  24.3 us (17%)
  local copies, waits for them, and re-layouts  13.3 us (10%)
  starting transfers between devices  11.9 us (9%)
  other arithmetic  4.46 us (3%)
    ppermute x6, waiting for transfers between devices, from_partner(): return lax.ppermute(block, axis, route)  74.9 us
    all_to_all x1, waiting for transfers between devices, per_device(): lax.all_to_all(jnp.stack([panel_y] * lax.axis_size('col')), 'col', 0, 0)  9.75 us
    ppermute x6, starting transfers between devices, from_partner(): return lax.ppermute(block, axis, route)  7.6 us
    dot_general x3, matrix products, pair_update(): return (first - factor, second - jnp.dot(vees, factor, precision=highest))  6.13 us
    dot_general x1, matrix products, per_device(): proj = jnp.einsum('mb,mn->bn', lower, trailing, precision=highest)  6 us
    dot_general x3, matrix products, pair_update(): factor = jnp.einsum('kb,kn->bn', tees, summed, precision=highest)  5.51 us
    unnamed x9, local copies, waits for them, and re-layouts  5.36 us
    concatenate x1, local copies, waits for them, and re-layouts, per_device(): return jnp.concatenate([top, rest], axis=0)  5.34 us
  transfers between devices with their start and end apart: 7, of which 7 were waited for; matrix products, arithmetic and copies ran while one was open for 4% of the time, Pallas kernels for 0%

profile of v1, /device:TPU:8, one launch (start us, length us, event | category | flops | bytes accessed | tf_op | source)
XLA Modules:
  0.0 138.8 jit_solution(10681230479417532072)
XLA Ops:
  0.0 2.0 %stack.2 = f32[4,256,256]{2,1,0:T(8,128)} broadcast(f32[256,256]{1,0:T(8,128)} %param.6), dimensions={1,2} | broadcast | bytes 1310720 | tf_op jit(solution)/shard_map/stack | solution.py:56
  2.0 4.3 %all-to-all-start = ((f32[4,256,256]{2,1,0:T(8,128)}), f32[4,256,256]{2,1,0:T(8,128)S(1)}, u32[]{:S(2)}, u32[]{:S(2)}) async-start(f32[4,256,256]{2,1,0:T(8,128)} %stack.2), calls=%async_computation | async-start | bytes 2097152 | tf_op jit(solution)/shard_map/all_to_all | solution.py:56
  6.3 5.3 %copy.6 = f32[1024,1024]{0,1:T(8,128)} copy(f32[1024,1024]{1,0:T(8,128)} %param.5) | data formatting | bytes 8388608 | tf_op args[0]
  11.6 9.8 %all-to-all-done = f32[4,256,256]{2,1,0:T(8,128)S(1)} async-done(((f32[4,256,256]{2,1,0:T(8,128)}), f32[4,256,256]{2,1,0:T(8,128)S(1)}, u32[]{:S(2)}, u32[]{:S(2)}) %all-to-all-start) | async-done | bytes 1048608 | tf_op jit(solution)/shard_map/all_to_all | solution.py:56
  21.5 6.0 %fusion.59 = f32[256,1024]{1,0:T(8,128)S(1)} fusion(f32[1024,256]{1,0:T(8,128)S(1)} %bitcast_select_fusion, f32[1024,1024]{1,0:T(8,128)} %param.5), kind=kOutput, calls=%fused_computation.94 | convolution fusion | flops 3221225472 | bytes 6291456 | tf_op jit(solution)/shard_map/mb,mn->bn/dot_general | solution.py:59
  27.5 1.1 fusion.12
  28.6 3.8 %convolution_subtract_fusion = f32[1024,1024]{0,1:T(8,128)S(1)} fusion(f32[1024,1024]{0,1:T(8,128)S(1)} %copy-done.1, f32[1024,256]{1,0:T(8,128)S(1)} %bitcast_select_fusion, f32[256,1024]{1,0:T(8,128)S(1)} %fusion.12), kind=kOutput, calls=%fused_computation.1 | convolution fusion | flops 3222274048 | bytes 10485760 | tf_op jit(solution)/shard_map/dot_general | solution.py:61
  32.6 1.9 %collective-permute-done = f32[256,512]{0,1:T(8,128)S(1)} collective-permute-done((f32[256,512]{0,1:T(8,128)S(1)}, f32[256,512]{0,1:T(8,128)S(1)}, u32[]{:S(2)}, u32[]{:S(2)}) %collective-permute-start) | collective-permute-done | bytes 524320 | tf_op jit(solution)/shard_map/ppermute | solution.py:15
  34.5 0.6 convolution_add_fusion.2
  35.1 1.8 %fusion.8 = f32[256,512]{1,0:T(8,128)S(1)} fusion(f32[256,512]{0,1:T(8,128)S(1)} %convolution_add_fusion.2, f32[3,256,256]{2,1,0:T(8,128)} %param.9), kind=kOutput, calls=%fused_computation.40 | convolution fusion | flops 403046400 | bytes 1310720 | tf_op jit(solution)/shard_map/kb,kn->bn/dot_general | solution.py:46
  37.0 0.2 copy.7
  37.2 3.0 %broadcast_select_fusion = (f32[256,512]{0,1:T(8,128)}, f32[256,512]{0,1:T(8,128)S(1)}, f32[256,512]{0,1:T(8,128)S(1)}) fusion(pred[]{:T(512)S(6)} %eq.100, f32[256,512]{0,1:T(8,128)S(1)} %copy.7, f32[256,512]{0,1:T(8,128)S(1)} %collective-permute-done, f32[1024,1024]{0,1:T(8,128)} %copy-done, f32[256,512]{1,0:T(8,128)S(1)} %fusion.8, ...), kind=kOutput, calls=%fused_computation.52 | convolution fusion | flops 403439616 | bytes 4456449 | tf_op jit(solution)/shard_map/dot_general | solution.py:47
  40.2 0.1 collective-permute-start.1
  40.3 2.0 %collective-permute-done.1 = f32[256,512]{0,1:T(8,128)S(1)} collective-permute-done((f32[256,512]{0,1:T(8,128)}, f32[256,512]{0,1:T(8,128)S(1)}, u32[]{:S(2)}, u32[]{:S(2)}) %collective-permute-start.1) | collective-permute-done | bytes 524320 | tf_op jit(solution)/shard_map/ppermute | solution.py:15
  42.5 2.2 %collective-permute-start.2 = (f32[256,512]{0,1:T(8,128)S(1)}, f32[256,512]{0,1:T(8,128)S(1)}, u32[]{:S(2)}, u32[]{:S(2)}) collective-permute-start(f32[256,512]{0,1:T(8,128)S(1)} %slice_select_fusion.4), channel_id=1, source_target_pairs={{0,8},{8,0},{4,12},{12,4},{16,24},{24,16},{20,28},{28,20},{32,40},... | collective-permute-start | bytes 1572872 | tf_op jit(solution)/shard_map/ppermute | solution.py:15
  44.7 12.2 %collective-permute-done.2 = f32[256,512]{0,1:T(8,128)S(1)} collective-permute-done((f32[256,512]{0,1:T(8,128)S(1)}, f32[256,512]{0,1:T(8,128)S(1)}, u32[]{:S(2)}, u32[]{:S(2)}) %collective-permute-start.2) | collective-permute-done | bytes 524320 | tf_op jit(solution)/shard_map/ppermute | solution.py:15
  56.9 0.6 convolution_add_fusion.1
  57.5 1.8 %fusion.5 = f32[256,512]{1,0:T(8,128)S(1)} fusion(f32[256,512]{0,1:T(8,128)S(1)} %convolution_add_fusion.1, f32[3,256,256]{2,1,0:T(8,128)} %param.9), kind=kOutput, calls=%fused_computation.34 | convolution fusion | flops 403046400 | bytes 1310720 | tf_op jit(solution)/shard_map/kb,kn->bn/dot_general | solution.py:46
  59.4 0.2 copy.9
  59.6 2.1 %broadcast_select_fusion.1 = (f32[256,512]{0,1:T(8,128)}, f32[256,512]{0,1:T(8,128)}, f32[256,512]{0,1:T(8,128)}) fusion(pred[]{:T(512)S(6)} %eq.99, f32[256,512]{0,1:T(8,128)S(1)} %copy.9, f32[256,512]{0,1:T(8,128)S(1)} %collective-permute-done.2, f32[256,1024]{0,1:T(8,128)S(1)} %maximum_select_fusion, f32[256,512]{1,0:T(8,128)S(1)} %fusion.5, ...), kind=kOutput, calls=%fused_computation.53 | convolution fusion | flops 403439616 | bytes 4456449 | tf_op jit(solution)/shard_map/dot_general | solution.py:47
  61.7 1.7 %collective-permute-start.3 = (f32[256,512]{0,1:T(8,128)}, f32[256,512]{0,1:T(8,128)S(1)}, u32[]{:S(2)}, u32[]{:S(2)}) collective-permute-start(f32[256,512]{0,1:T(8,128)} %get-tuple-element.7), channel_id=1, source_target_pairs={{0,8},{8,0},{4,12},{12,4},{16,24},{24,16},{20,28},{28,20},{32,40},... | collective-permute-start | bytes 1572872 | tf_op jit(solution)/shard_map/ppermute | solution.py:15
  63.4 11.7 %collective-permute-done.3 = f32[256,512]{0,1:T(8,128)S(1)} collective-permute-done((f32[256,512]{0,1:T(8,128)}, f32[256,512]{0,1:T(8,128)S(1)}, u32[]{:S(2)}, u32[]{:S(2)}) %collective-permute-start.3) | collective-permute-done | bytes 524320 | tf_op jit(solution)/shard_map/ppermute | solution.py:15
  75.2 1.3 maximum_select_fusion.1
  76.5 3.4 %collective-permute-start.4 = (f32[256,512]{0,1:T(8,128)S(1)}, f32[256,512]{0,1:T(8,128)S(1)}, u32[]{:S(2)}, u32[]{:S(2)}) collective-permute-start(f32[256,512]{0,1:T(8,128)S(1)} %slice_select_fusion.1), channel_id=1, source_target_pairs={{0,16},{16,0},{4,20},{20,4},{8,24},{24,8},{12,28},{28,12},{32,48},... | collective-permute-start | bytes 1572872 | tf_op jit(solution)/shard_map/ppermute | solution.py:15
  79.9 21.9 %collective-permute-done.4 = f32[256,512]{0,1:T(8,128)S(1)} collective-permute-done((f32[256,512]{0,1:T(8,128)S(1)}, f32[256,512]{0,1:T(8,128)S(1)}, u32[]{:S(2)}, u32[]{:S(2)}) %collective-permute-start.4) | collective-permute-done | bytes 524320 | tf_op jit(solution)/shard_map/ppermute | solution.py:15
  101.8 0.6 convolution_add_fusion
  102.4 1.8 %fusion.2 = f32[256,512]{1,0:T(8,128)S(1)} fusion(f32[256,512]{0,1:T(8,128)S(1)} %convolution_add_fusion, f32[3,256,256]{2,1,0:T(8,128)} %param.9), kind=kOutput, calls=%fused_computation.28 | convolution fusion | flops 403046400 | bytes 1310720 | tf_op jit(solution)/shard_map/kb,kn->bn/dot_general | solution.py:46
  104.3 0.2 copy.11
  104.5 1.0 broadcast_select_fusion.2
  105.6 25.1 %collective-permute-done.5 = f32[256,512]{0,1:T(8,128)S(1)} collective-permute-done((f32[256,512]{0,1:T(8,128)S(1)}, f32[256,512]{0,1:T(8,128)S(1)}, u32[]{:S(2)}, u32[]{:S(2)}) %collective-permute-start.5) | collective-permute-done | bytes 524320 | tf_op jit(solution)/shard_map/ppermute | solution.py:15
  130.9 2.6 %pad_maximum_fusion = f32[1024,1024]{0,1:T(8,128)} fusion(f32[768,1024]{0,1:T(8,128)S(1)} %slice-done, f32[256,1024]{0,1:T(8,128)S(1)} %maximum_select_fusion.2), kind=kLoop, calls=%fused_computation | loop fusion | flops 1048576 | bytes 8388608 | tf_op jit(solution)/shard_map/concatenate | solution.py:83
  133.5 5.3 %copy.13 = f32[1024,1024]{1,0:T(8,128)} copy(f32[1024,1024]{0,1:T(8,128)} %pad_maximum_fusion) | data formatting | bytes 8388608 | tf_op jit(solution)/shard_map/concatenate | solution.py:83
  (18 shorter events, 0.8 us)
Async XLA Ops:
  2.0 19.4 %all-to-all-start = ((f32[4,256,256]{2,1,0:T(8,128)}), f32[4,256,256]{2,1,0:T(8,128)S(1)}, u32[]{:S(2)}, u32[]{:S(2)}) async-start(f32[4,256,256]{2,1,0:T(8,128)} %stack.2), calls=%async_computation | async-start | bytes 2097152 | tf_op jit(solution)/shard_map/all_to_all | solution.py:56
  11.6 15.9 %copy-start.3 = (f32[256,256]{1,0:T(8,128)S(1)}, f32[256,256]{1,0:T(8,128)}, u32[]{:S(2)}) copy-start(f32[256,256]{1,0:T(8,128)} %param.7) | copy-start | bytes 786436
  21.5 7.1 %copy-start.1 = (f32[1024,1024]{0,1:T(8,128)S(1)}, f32[1024,1024]{0,1:T(8,128)}, u32[]{:S(2)}) copy-start(f32[1024,1024]{0,1:T(8,128)} %copy.6) | copy-start | bytes 12582916
  28.6 5.9 %copy-start.2 = (f32[3,256,256]{2,1,0:T(8,128)S(1)}, f32[3,256,256]{2,1,0:T(8,128)}, u32[]{:S(2)}) copy-start(f32[3,256,256]{2,1,0:T(8,128)} %param.8) | copy-start | bytes 2359300
  32.4 2.1 %copy-start = (f32[1024,1024]{0,1:T(8,128)}, f32[1024,1024]{0,1:T(8,128)S(1)}, u32[]{:S(2)}) copy-start(f32[1024,1024]{0,1:T(8,128)S(1)} %convolution_subtract_fusion) | copy-start | bytes 12582916
  32.5 2.0 %collective-permute-start = (f32[256,512]{0,1:T(8,128)S(1)}, f32[256,512]{0,1:T(8,128)S(1)}, u32[]{:S(2)}, u32[]{:S(2)}) collective-permute-start(f32[256,512]{0,1:T(8,128)S(1)} %slice_select_fusion.7), channel_id=1, source_target_pairs={{0,4},{4,0},{8,12},{12,8},{16,20},{20,16},{24,28},{28,24},{32,36},... | collective-permute-start | bytes 1572872 | tf_op jit(solution)/shard_map/ppermute | solution.py:15
  40.2 2.1 %collective-permute-start.1 = (f32[256,512]{0,1:T(8,128)}, f32[256,512]{0,1:T(8,128)S(1)}, u32[]{:S(2)}, u32[]{:S(2)}) collective-permute-start(f32[256,512]{0,1:T(8,128)} %get-tuple-element.9), channel_id=1, source_target_pairs={{0,4},{4,0},{8,12},{12,8},{16,20},{20,16},{24,28},{28,24},{32,36},... | collective-permute-start | bytes 1572872 | tf_op jit(solution)/shard_map/ppermute | solution.py:15
  42.5 14.4 %collective-permute-start.2 = (f32[256,512]{0,1:T(8,128)S(1)}, f32[256,512]{0,1:T(8,128)S(1)}, u32[]{:S(2)}, u32[]{:S(2)}) collective-permute-start(f32[256,512]{0,1:T(8,128)S(1)} %slice_select_fusion.4), channel_id=1, source_target_pairs={{0,8},{8,0},{4,12},{12,4},{16,24},{24,16},{20,28},{28,20},{32,40},... | collective-permute-start | bytes 1572872 | tf_op jit(solution)/shard_map/ppermute | solution.py:15
  61.7 13.5 %collective-permute-start.3 = (f32[256,512]{0,1:T(8,128)}, f32[256,512]{0,1:T(8,128)S(1)}, u32[]{:S(2)}, u32[]{:S(2)}) collective-permute-start(f32[256,512]{0,1:T(8,128)} %get-tuple-element.7), channel_id=1, source_target_pairs={{0,8},{8,0},{4,12},{12,4},{16,24},{24,16},{20,28},{28,20},{32,40},... | collective-permute-start | bytes 1572872 | tf_op jit(solution)/shard_map/ppermute | solution.py:15
  76.5 25.3 %collective-permute-start.4 = (f32[256,512]{0,1:T(8,128)S(1)}, f32[256,512]{0,1:T(8,128)S(1)}, u32[]{:S(2)}, u32[]{:S(2)}) collective-permute-start(f32[256,512]{0,1:T(8,128)S(1)} %slice_select_fusion.1), channel_id=1, source_target_pairs={{0,16},{16,0},{4,20},{20,4},{8,24},{24,8},{12,28},{28,12},{32,48},... | collective-permute-start | bytes 1572872 | tf_op jit(solution)/shard_map/ppermute | solution.py:15
  105.5 25.3 %slice-start = ((f32[1024,1024]{0,1:T(8,128)}), f32[768,1024]{0,1:T(8,128)S(1)}, s32[]{:S(2)}) async-start(f32[1024,1024]{0,1:T(8,128)} %copy-done), calls=%async_computation.1 | async-start | bytes 6291456 | tf_op jit(solution)/shard_map/slice | solution.py:63
  105.5 25.2 %collective-permute-start.5 = (f32[256,512]{0,1:T(8,128)S(1)}, f32[256,512]{0,1:T(8,128)S(1)}, u32[]{:S(2)}, u32[]{:S(2)}) collective-permute-start(f32[256,512]{0,1:T(8,128)S(1)} %get-tuple-element.5), channel_id=1, source_target_pairs={{0,16},{16,0},{4,20},{20,4},{8,24},{24,8},{12,28},{28,12},{32,48},... | collective-permute-start | bytes 1572872 | tf_op jit(solution)/shard_map/ppermute | solution.py:15
